TPU v7x, 32 devices: a whole 2x2x4 slice. The times are simulated.
32 devices in a mesh: stream: 8 (over z, x), cross: 4 (over y, core).
Axes of the slice: x: 2, y: 2, z: 4, core: 2. Of those that a mesh axis runs over, the one named last changes fastest.
Arguments:
- rhs: float32 [128, 320, 128], P(('stream', 'cross')), may hold values from -240 to 240
- damping: float32 [128, 320], P(('stream', 'cross')), may hold values from 3 to 6
- omega: float32 [1], replicated, may hold values from 1 to 3
- jac_diag: bfloat16 [128, 320, 320], P(('stream', 'cross')), may hold values from -0.15625 to 0.15625
- jac_face: bfloat16 [128, 320, 480], P(('stream', 'cross')), may hold values from -0.125 to 0.125
- face_list: int32 [128, 6], P(('stream', 'cross')), may hold values from 0 to 36, as said below
- stream_sends: int32 [32, 2, 4], P(('stream', 'cross')), may hold values from 0 to 19, as said below
- cross_sends: int32 [32, 2, 2], P(('stream', 'cross')), may hold values from 0 to 23, as said below
Outputs:
- solution: float32 [128, 320, 128], P(('stream', 'cross'))
- residual: float32 [128, 320, 128], P(('stream', 'cross'))
Inputs may be any that keep to these rules, and one draw needn't show every extreme that they name: `face_list`: within each partition, each face of an element points to the opposite face of its neighbour: to a slot 6 e + f of an own element, to a received trace in the layout of the table, or to the zero last slot on radial boundaries. Every received slot is read by exactly one face. `stream_sends`: each row lists distinct own trace slots 6 e + f of streamwise faces, in the order in which the neighbour's table receives them. `cross_sends`: each row lists distinct own trace slots 6 e + f of azimuthal faces, in the order in which the neighbour's table receives them; the cross partitions close into a loop.
All inputs are finite; a program needn't handle non-finite values.
Results may differ from a plain program's by a relative error of at most 0.003.
The roundings to bfloat16 on the way count: a program that leaves them out, or rounds other values in their place, can miss the bound.
Values may be sent and summed in bfloat16 or wider, within the bound.
No kernel may reach another device: no remote copies, remote signals or barrier semaphores. Data moves between devices by JAX's collectives and lax.ppermute only.
A program may use at most 128 MiB of HBM per device.

v0:
```python
import jax
import jax.numpy as jnp
import numpy as np
from jax import lax
from jax.sharding import PartitionSpec as P

NP = 4
NVAR = 5
ITERS = 3


def passed_along(value, axis, steps):
    count = lax.axis_size(axis)
    first, last = (max(0, -steps), min(count, count - steps))
    return lax.ppermute(value, axis, [(source, source + steps) for source in range(first, last)])


def shifted(block, axis, distance):
    devices = range(lax.axis_size(axis))
    route = [((i - distance) % len(devices), i) for i in devices]
    return lax.ppermute(block, axis, route)


def inner(left, right):
    width = left.shape[-1] // 2
    return lax.dot_general(
        left.reshape(-1, width),
        right.reshape(-1, width),
        (((0,), (0,)), ((), ())),
        precision=lax.Precision.HIGHEST,
        preferred_element_type=jnp.float32,
    )


def combine(field, matrix):
    width = matrix.shape[0]
    flat = field.reshape(-1, width)
    return jnp.dot(
        flat, matrix, precision=lax.Precision.HIGHEST, preferred_element_type=jnp.float32
    ).reshape(field.shape)


def small_dot(left, right):
    return jnp.dot(left, right, precision=lax.Precision.HIGHEST, preferred_element_type=jnp.float32)


def orthonormal(field, gram):
    lower = jnp.linalg.cholesky(gram)
    inverse = lax.linalg.triangular_solve(
        lower, jnp.eye(gram.shape[0], dtype=gram.dtype), left_side=True, lower=True
    )
    return (combine(field, inverse.T), lower.T)


def face_rows():
    grid = np.arange(NVAR * NP * NP * NP).reshape(NVAR, NP, NP, NP)
    faces = [
        grid[:, 0],
        grid[:, NP - 1],
        grid[:, :, 0],
        grid[:, :, NP - 1],
        grid[:, :, :, 0],
        grid[:, :, :, NP - 1],
    ]
    return np.concatenate([item.reshape(-1) for item in faces]).astype(np.int32)


def face_traces(rounded):
    count = rounded.shape[0]
    columns = rounded.shape[-1]
    picked = jnp.take(rounded, jnp.asarray(face_rows()), axis=1)
    return picked.reshape(count * 6, NVAR * NP * NP, columns)


def rotate(field):
    half = field.shape[-1] // 2
    return jnp.concatenate([-field[..., half:], field[..., :half]], axis=-1)


def start_block(rhs):
    width = rhs.shape[-1] // 2
    real_part = rhs[..., :width]
    imag_part = rhs[..., width:]
    return jnp.concatenate([real_part, -imag_part, imag_part, real_part], axis=-1)


def least_squares(hessenberg, first_upper):
    height = hessenberg.shape[0]
    width = first_upper.shape[0]
    target = jnp.zeros((height, width), first_upper.dtype).at[:width].set(first_upper)
    normal = small_dot(hessenberg.T, hessenberg)
    right = small_dot(hessenberg.T, target)
    lower = jnp.linalg.cholesky(normal)
    middle = lax.linalg.triangular_solve(lower, right, left_side=True, lower=True)
    coeffs = lax.linalg.triangular_solve(
        lower, middle, left_side=True, lower=True, transpose_a=True
    )
    leftover = target - small_dot(hessenberg, coeffs)
    return (coeffs, leftover)


def lengths_sum(field):
    return lax.psum(inner(field, field), ("stream", "cross"))


def body(rhs, damping, omega, jac_diag, jac_face, face_list, stream_sends, cross_sends):
    count = rhs.shape[0]
    blocksize = rhs.shape[-1]
    columns = 2 * blocksize
    listing = face_list.reshape(-1)
    block = start_block(rhs)
    first, first_upper = orthonormal(block, lengths_sum(block))
    basis = [first]
    hessenberg = jnp.zeros(((ITERS + 1) * blocksize, ITERS * blocksize), jnp.float32)
    for step in range(ITERS):
        field = basis[step]
        rounded = field.astype(jnp.bfloat16)
        traces = face_traces(rounded)
        stream_pack = traces[stream_sends[0]]
        cross_pack = traces[cross_sends[0]]
        from_prev = passed_along(stream_pack[0], "stream", 1)
        from_next = passed_along(stream_pack[1], "stream", -1)
        cross_prev = shifted(cross_pack[0], "cross", 1)
        cross_next = shifted(cross_pack[1], "cross", -1)
        interior = jnp.einsum("eij,ejc->eic", jac_diag, rounded, preferred_element_type=jnp.float32)
        zero_slot = jnp.zeros((1,) + traces.shape[1:], traces.dtype)
        table = jnp.concatenate(
            [traces, from_prev, from_next, cross_prev, cross_next, zero_slot], axis=0
        )
        gathered = table[listing].reshape(count, -1, columns)
        coupled = jnp.einsum("eik,ekc->eic", jac_face, gathered, preferred_element_type=jnp.float32)
        image = interior + coupled + damping[:, :, None] * field + omega[0] * rotate(field)
        local = jnp.stack([inner(vector, image) for vector in basis])
        coeffs = lax.psum(local, ("stream", "cross"))
        for number, vector in enumerate(basis):
            image = image - combine(vector, coeffs[number])
        gram = lengths_sum(image)
        fresh, upper = orthonormal(image, gram)
        for number in range(step + 1):
            hessenberg = hessenberg.at[
                number * blocksize : (number + 1) * blocksize,
                step * blocksize : (step + 1) * blocksize,
            ].set(coeffs[number])
        hessenberg = hessenberg.at[
            (step + 1) * blocksize : (step + 2) * blocksize,
            step * blocksize : (step + 1) * blocksize,
        ].set(upper)
        basis.append(fresh)
    weights, leftover = least_squares(hessenberg, first_upper)
    result = combine(basis[0], weights[:blocksize])
    for step in range(1, ITERS):
        result = result + combine(basis[step], weights[step * blocksize : (step + 1) * blocksize])
    remain = combine(basis[0], leftover[:blocksize])
    for step in range(1, ITERS + 1):
        remain = remain + combine(basis[step], leftover[step * blocksize : (step + 1) * blocksize])
    width = blocksize // 2
    solution = jnp.concatenate(
        [result[..., :width], result[..., blocksize : blocksize + width]], axis=-1
    )
    residual = jnp.concatenate(
        [remain[..., :width], remain[..., blocksize : blocksize + width]], axis=-1
    )
    return (solution, residual)


def solution(mesh):
    in_specs = (
        P(("stream", "cross"), None, None),
        P(("stream", "cross"), None),
        P(),
        P(("stream", "cross"), None, None),
        P(("stream", "cross"), None, None),
        P(("stream", "cross"), None),
        P(("stream", "cross"), None, None),
        P(("stream", "cross"), None, None),
    )
    out_specs = (P(("stream", "cross"), None, None), P(("stream", "cross"), None, None))
    return jax.shard_map(body, mesh=mesh, in_specs=in_specs, out_specs=out_specs, check_vma=False)
```

profile of v0, /device:TPU:1, one launch (start us, length us, event | category | flops | bytes accessed | tf_op | source)
XLA Modules:
  0.0 1384.4 jit_solution(1808762299347239370)
XLA Ops:
  11.9 2.9 fusion.101
  17.7 120.6 %all-reduce.11.cloned.1.call-done = f32[128,128]{0,1:T(8,128)} async-done(((f32[128,128]{0,1:T(8,128)}), f32[128,128]{0,1:T(8,128)}) %all-reduce.11.cloned.1.call-update) | async-done | bytes 65552 | tf_op jit(solution)/shard_map/psum | solution.py:103
  140.1 11.7 cholesky.237
  153.2 9.8 custom-call.35
  171.4 3.8 gather_fusion.9
  181.7 3.7 collective-permute-start
  189.1 2.9 fusion.113
  198.8 3.0 gather_fusion.2
  201.9 3.8 fusion.8
  208.1 4.2 fusion.103
  212.9 121.7 %all-reduce.13.cloned.1.call-done = f32[128,128]{1,0:T(8,128)} async-done(((f32[128,128]{1,0:T(8,128)}), f32[128,128]{1,0:T(8,128)}) %all-reduce.13.cloned.1.call-update) | async-done | bytes 65552 | tf_op jit(solution)/shard_map/psum | solution.py:134
  334.7 3.1 fusion.104
  340.4 2.9 sub.21
  345.7 4.6 fusion.105
  351.1 120.0 %all-reduce.15.cloned.1.call-done = f32[128,128]{0,1:T(8,128)} async-done(((f32[128,128]{0,1:T(8,128)}), f32[128,128]{0,1:T(8,128)}) %all-reduce.15.cloned.1.call-update) | async-done | bytes 65552 | tf_op jit(solution)/shard_map/psum | solution.py:103
  473.5 12.5 cholesky.248
  489.5 11.3 custom-call.36
  501.9 3.6 fusion.106
  511.6 3.8 gather_fusion.10
  522.7 3.1 fusion.114
  527.8 3.7 collective-permute-start.4
  544.7 3.1 gather_fusion.5
  547.8 4.1 fusion.5
  554.3 3.7 convolution_bitcast_fusion.4
  561.0 123.1 %all-reduce.17.cloned.1.call-done = f32[2,128,128]{2,1,0:T(8,128)} async-done(((f32[2,128,128]{2,1,0:T(8,128)}), f32[2,128,128]{2,1,0:T(8,128)}) %all-reduce.17.cloned.1.call-update) | async-done | bytes 131088 | tf_op jit(solution)/shard_map/psum | solution.py:134
  684.1 3.1 fusion.68
  689.8 3.6 fusion.69
  696.0 3.5 subtract_subtract_fusion.1
  701.8 4.6 fusion.107
  706.7 2.8 dynamic-slice_select_fusion.1
  709.5 2.9 scatter.36
  713.3 114.4 %all-reduce.19.cloned.1.call-done = f32[128,128]{0,1:T(8,128)} async-done(((f32[128,128]{0,1:T(8,128)}), f32[128,128]{0,1:T(8,128)}) %all-reduce.19.cloned.1.call-update) | async-done | bytes 65552 | tf_op jit(solution)/shard_map/psum | solution.py:103
  830.2 12.5 cholesky.259
  846.1 11.3 custom-call.37
  858.5 3.6 fusion.108
  862.1 2.7 reshape.560
  868.3 3.7 gather_fusion.11
  879.4 3.1 fusion.115
  884.4 3.7 collective-permute-start.8
  901.3 3.1 gather_fusion.8
  904.4 4.1 fusion.2
  910.9 3.7 convolution_bitcast_fusion.2
  920.3 123.1 %all-reduce.21.cloned.1.call-done = f32[3,128,128]{2,1,0:T(8,128)} async-done(((f32[3,128,128]{2,1,0:T(8,128)}), f32[3,128,128]{2,1,0:T(8,128)}) %all-reduce.21.cloned.1.call-update) | async-done | bytes 196624 | tf_op jit(solution)/shard_map/psum | solution.py:134
  1043.3 3.1 fusion.71
  1046.4 2.7 reshape.569
  1049.1 3.6 fusion.72
  1055.3 3.6 fusion.74
  1058.9 2.7 reshape.571
  1061.6 4.0 subtract_subtract_fusion
  1068.0 4.6 fusion.109
  1072.7 2.8 dynamic-slice_select_fusion
  1079.8 115.8 %all-reduce.23.cloned.1.call-done = f32[128,128]{0,1:T(8,128)} async-done(((f32[128,128]{0,1:T(8,128)}), f32[128,128]{0,1:T(8,128)}) %all-reduce.23.cloned.1.call-update) | async-done | bytes 65552 | tf_op jit(solution)/shard_map/psum | solution.py:103
  1198.1 12.5 cholesky.270
  1220.7 12.5 cholesky.87
  1234.7 10.6 custom-call.29
  1249.5 12.3 cholesky.160
  1264.5 10.4 custom-call.30
  1278.6 12.5 cholesky.179
  1296.1 10.2 while.11
  1296.7 2.8 bitcast_dynamic-update-slice_fusion.2
  1300.1 2.8 bitcast_dynamic-update-slice_fusion.2
  1303.5 2.7 bitcast_dynamic-update-slice_fusion.2
  1306.2 31.1 %custom-call.31 = f32[3,128,128]{1,2,0:T(8,128)} custom-call(f32[3,128,128]{2,1,0:T(8,128)} %get-tuple-element.132), custom_call_target="InvertDiagBlocksLowerTriangular" | custom-call | tf_op jit(solution)/shard_map/triangular_solve | solution.py:95
  1347.2 10.6 custom-call.38
  (295 shorter events, 202.5 us)
Async XLA Ops:
  7.2 194.7 %copy-start = (bf16[4,320,480]{2,1,0:T(8,128)(2,1)S(1)}, bf16[4,320,480]{2,1,0:T(8,128)(2,1)}, u32[]{:S(2)}) copy-start(bf16[4,320,480]{2,1,0:T(8,128)(2,1)} %param.40) | copy-start | bytes 3686404
  7.2 131.1 %all-reduce.11.cloned.1.call-start = ((), (), s32[]{:S(2)}) async-start(), calls=%async_computation | async-start | bytes 131072 | tf_op jit(solution)/shard_map/psum | solution.py:103
  11.9 2.9 copy-start.11
  11.9 3.5 copy-start.42
  11.9 3.5 copy-start.44
  11.9 3.6 copy-start.45
  11.9 3.7 copy-start.43
  11.9 4.4 copy-start.47
  14.8 319.8 %all-reduce.13.cloned.1.call-start = ((), (), s32[]{:S(2)}) async-start(), calls=%async_computation.1 | async-start | bytes 131072 | tf_op jit(solution)/shard_map/psum | solution.py:134
  15.7 183.1 %copy-start.41 = (s32[1024]{0:T(1024)}, s32[1024]{0:T(1024)S(1)}, u32[]{:S(2)}) copy-start(s32[1024]{0:T(1024)S(1)} %pad_clamp_fusion) | copy-start | bytes 12292
  17.0 160.4 %copy-start.40 = (s32[1024]{0:T(1024)}, s32[1024]{0:T(1024)S(1)}, u32[]{:S(2)}) copy-start(s32[1024]{0:T(1024)S(1)} %get-tuple-element.192) | copy-start | bytes 12292
  153.1 1184.2 %copy-start.31 = (f32[128,128]{0,1:T(8,128)}, f32[128,128]{0,1:T(8,128)S(1)}, u32[]{:S(2)}) copy-start(f32[128,128]{0,1:T(8,128)S(1)} %get-tuple-element.179) | copy-start | bytes 196612
  167.2 1.7 copy-start.10
  181.7 12.0 collective-permute-start
  185.4 9.9 collective-permute-start.1
  189.1 2.9 copy-start.30
  189.1 2.9 copy-start.16
  193.0 3.9 collective-permute-start.2
  193.2 4.4 collective-permute-start.3
  195.3 6.6 copy-start.22
  195.3 6.6 copy-start.39
  212.3 258.8 %all-reduce.15.cloned.1.call-start = ((), (), s32[]{:S(2)}) async-start(), calls=%async_computation.2 | async-start | bytes 131072 | tf_op jit(solution)/shard_map/psum | solution.py:103
  345.7 5.4 copy-start.38
  350.3 333.8 %all-reduce.17.cloned.1.call-start = ((), (), s32[]{:S(2)}) async-start(), calls=%async_computation.3 | async-start | bytes 262144 | tf_op jit(solution)/shard_map/psum | solution.py:134
  509.4 0.8 copy-start.18
  522.7 3.1 copy-start.9
  525.9 1.2 copy-start.25
  525.9 6.9 copy-start.29
  525.9 7.6 copy-start.15
  527.8 8.4 collective-permute-start.4
  531.5 8.0 collective-permute-start.5
  534.5 6.5 collective-permute-start.6
  534.7 7.9 collective-permute-start.7
  554.3 3.7 copy-start.1
  554.3 3.7 copy-start.13
  558.0 3.0 copy-start.37
  560.9 266.8 %all-reduce.19.cloned.1.call-start = ((), (), s32[]{:S(2)}) async-start(), calls=%async_computation.4 | async-start | bytes 131072 | tf_op jit(solution)/shard_map/psum | solution.py:103
  706.5 336.8 %all-reduce.21.cloned.1.call-start = ((), (), s32[]{:S(2)}) async-start(), calls=%async_computation.5 | async-start | bytes 393216 | tf_op jit(solution)/shard_map/psum | solution.py:134
  866.2 0.8 copy-start.17
  879.4 3.1 copy-start.8
  882.5 1.2 copy-start.24
  882.5 6.9 copy-start.28
  882.5 7.6 copy-start.14
  884.4 8.2 collective-permute-start.8
  888.1 7.9 collective-permute-start.9
  891.1 6.5 collective-permute-start.10
  891.3 7.9 collective-permute-start.11
  910.9 3.7 copy-start.2
  910.9 3.7 copy-start.12
  914.6 2.2 copy-start.5
  916.9 3.4 copy-start.36
  919.8 275.8 %all-reduce.23.cloned.1.call-start = ((), (), s32[]{:S(2)}) async-start(), calls=%async_computation.6 | async-start | bytes 131072 | tf_op jit(solution)/shard_map/psum | solution.py:103
  1219.2 0.8 copy-start.23
  1247.2 48.9 %copy-start.46 = (s32[3]{0:T(128)S(1)}, s32[3]{0:T(128)}, u32[]{:S(2)}) copy-start(s32[3]{0:T(128)} %iota_multiply_fusion) | copy-start | bytes 40
  1337.3 3.7 copy-start.27
  1337.3 4.0 copy-start.20
  1338.8 4.4 copy-start.32
  1358.1 2.6 copy-start.26
  1360.7 1.3 copy-start.3
  1362.0 1.3 copy-start.6
  1367.4 2.4 copy-start.4
  1367.4 2.4 copy-start.19
  1369.8 1.3 copy-start.7
  1373.7 1.5 copy-start.21
  (3 other events, 1.9 us)
Sparse Core Ops, SparseCore 0:
  14.9 123.3 all-reduce.10
  212.4 122.2 all-reduce.12
  350.5 120.5 all-reduce.14
  561.0 123.0 all-reduce.16
  706.6 121.0 all-reduce.18
  919.9 123.3 all-reduce.20
  1072.8 122.8 all-reduce.22
where the time goes:
time: 1390 us; the launch traced here: 1380 us
  waiting for transfers between devices  842 us (61%)
  other arithmetic  236 us (17%)
  local copies, waits for them, and re-layouts  152 us (11%)
  matrix products  117 us (8%)
  starting transfers between devices  18.9 us (1%)
  between operations  17.7 us (1%)
    psum x4, waiting for transfers between devices, lengths_sum(): return lax.psum(inner(field, field), ('stream', 'cross'))  471 us
    psum x3, waiting for transfers between devices, body(): coeffs = lax.psum(local, ('stream', 'cross'))  368 us
    another operation x11, other arithmetic, least_squares(): lower = jnp.linalg.cholesky(normal)  63.1 us
    another operation x12, other arithmetic, orthonormal(): lower = jnp.linalg.cholesky(gram)  52 us
    another operation x7, other arithmetic, orthonormal(): lax.linalg.triangular_solve(lower, jnp.eye(gram.shape[0], dtype=gram.dtyp...  48.6 us
    dot_general x17, matrix products, combine(): jnp.dot(flat, matrix, precision=lax.Precision.HIGHEST, preferred_element_...  41.9 us
    dot_general x10, matrix products, inner(): lax.dot_general(left.reshape(-1, width), right.reshape(-1, width), (((0,)...  34.9 us
    another operation x3, other arithmetic, least_squares(): lax.linalg.triangular_solve(lower, middle, left_side=True, lower=True, tr...  33.5 us
  transfers between devices with their start and end apart: 19, of which 9 were waited for; matrix products, arithmetic and copies ran while one was open for 3% of the time, Pallas kernels for 0%

commit v1 on v0

--- a/solution.py
+++ b/solution.py
@@ -100,7 +100,7 @@
 
 
 def lengths_sum(field):
-    return lax.psum(inner(field, field), ("stream", "cross"))
+    return jnp.sum(lax.all_gather(inner(field, field), ("stream", "cross")), axis=0)
 
 
 def body(rhs, damping, omega, jac_diag, jac_face, face_list, stream_sends, cross_sends):

time: 1390 us -> 1130 us (0.81)
  waiting for transfers between devices: 842 us -> 581 us
    psum x4 -> x0, waiting for transfers between devices: 471 us -> none  [lengths_sum(): return lax.psum(inner(field, field), ('stream', 'cross'))]
    all_gather x0 -> x4, waiting for transfers between devices: none -> 203 us  [lengths_sum(): lax.all_gather(inner(field, field), ('stream', 'cross'))]
  transfers between devices with their start and end apart: 19 -> 19, of which waited for: 9 -> 9; matrix products, arithmetic and copies ran while one was open for 3% -> 4% of each run, Pallas kernels for 0% -> 0%
where the time goes in v1:
time: 1130 us; the launch traced here: 1120 us
  waiting for transfers between devices  581 us (51%)
  other arithmetic  241 us (21%)
  local copies, waits for them, and re-layouts  145 us (13%)
  matrix products  115 us (10%)
  starting transfers between devices  18.4 us (2%)
  between operations  17.8 us (2%)
    psum x3, waiting for transfers between devices, body(): coeffs = lax.psum(local, ('stream', 'cross'))  372 us
    all_gather x4, waiting for transfers between devices, lengths_sum(): lax.all_gather(inner(field, field), ('stream', 'cross'))  203 us
    another operation x11, other arithmetic, least_squares(): lower = jnp.linalg.cholesky(normal)  68.5 us
    another operation x12, other arithmetic, orthonormal(): lower = jnp.linalg.cholesky(gram)  51.9 us
    another operation x7, other arithmetic, orthonormal(): lax.linalg.triangular_solve(lower, jnp.eye(gram.shape[0], dtype=gram.dtyp...  44.8 us
    dot_general x17, matrix products, combine(): jnp.dot(flat, matrix, precision=lax.Precision.HIGHEST, preferred_element_...  41.9 us
    dot_general x10, matrix products, inner(): lax.dot_general(left.reshape(-1, width), right.reshape(-1, width), (((0,)...  34.8 us
    another operation x3, other arithmetic, least_squares(): lax.linalg.triangular_solve(lower, middle, left_side=True, lower=True, tr...  33 us
  transfers between devices with their start and end apart: 19, of which 9 were waited for; matrix products, arithmetic and copies ran while one was open for 4% of the time, Pallas kernels for 0%

profile of v1, /device:TPU:1, one launch (start us, length us, event | category | flops | bytes accessed | tf_op | source)
XLA Modules:
  0.0 1118.2 jit_solution(8267456087667890245)
XLA Ops:
  11.9 2.9 fusion.101
  16.4 57.3 %all-gather.9.cloned.1.call-done = f32[4096,128]{1,0:T(8,128)} async-done(((f32[128,128]{1,0:T(8,128)}), f32[4096,128]{1,0:T(8,128)}) %all-gather.9.cloned.1.call-update) | async-done | bytes 2097168 | tf_op jit(solution)/shard_map/all_gather | solution.py:103
  75.5 11.7 %cholesky.237 = f32[128,128]{1,0:T(8,128)S(1)} custom-call(f32[128,128]{1,0:T(8,128)S(1)} %fusion.56), custom_call_target="Cholesky" | custom-call | tf_op jit(solution)/shard_map/jit(cholesky)/cholesky | solution.py:48
  88.5 9.8 custom-call.35
  106.8 3.8 gather_fusion.9
  117.1 3.7 collective-permute-start
  123.9 2.9 fusion.113
  133.9 3.0 gather_fusion.2
  136.9 3.9 fusion.8
  143.1 4.2 fusion.103
  147.4 122.5 %all-reduce.7.cloned.1.call-done = f32[128,128]{1,0:T(8,128)} async-done(((f32[128,128]{1,0:T(8,128)}), f32[128,128]{1,0:T(8,128)}) %all-reduce.7.cloned.1.call-update) | async-done | bytes 65552 | tf_op jit(solution)/shard_map/psum | solution.py:134
  269.9 3.1 fusion.104
  275.6 3.0 sub.21
  280.9 4.6 fusion.105
  285.8 55.9 %all-gather.11.cloned.1.call-done = f32[4096,128]{1,0:T(8,128)} async-done(((f32[128,128]{1,0:T(8,128)}), f32[4096,128]{1,0:T(8,128)}) %all-gather.11.cloned.1.call-update) | async-done | bytes 2097168 | tf_op jit(solution)/shard_map/all_gather | solution.py:103
  343.5 11.7 %cholesky.248 = f32[128,128]{1,0:T(8,128)S(1)} custom-call(f32[128,128]{1,0:T(8,128)S(1)} %fusion.54), custom_call_target="Cholesky" | custom-call | tf_op jit(solution)/shard_map/jit(cholesky)/cholesky | solution.py:48
  357.1 9.8 custom-call.36
  367.2 3.6 fusion.106
  376.2 3.7 gather_fusion.10
  386.5 2.9 fusion.114
  390.4 3.1 collective-permute-start.4
  397.6 2.9 collective-permute-done.5
  403.1 3.0 gather_fusion.5
  406.1 3.8 fusion.5
  412.3 3.7 convolution_bitcast_fusion.4
  419.0 124.8 %all-reduce.9.cloned.1.call-done = f32[2,128,128]{2,1,0:T(8,128)} async-done(((f32[2,128,128]{2,1,0:T(8,128)}), f32[2,128,128]{2,1,0:T(8,128)}) %all-reduce.9.cloned.1.call-update) | async-done | bytes 131088 | tf_op jit(solution)/shard_map/psum | solution.py:134
  543.7 3.1 fusion.68
  549.5 3.6 fusion.69
  555.7 3.5 subtract_subtract_fusion.1
  561.6 4.6 fusion.107
  566.4 56.4 %all-gather.13.cloned.1.call-done = f32[4096,128]{1,0:T(8,128)} async-done(((f32[128,128]{1,0:T(8,128)}), f32[4096,128]{1,0:T(8,128)}) %all-gather.13.cloned.1.call-update) | async-done | bytes 2097168 | tf_op jit(solution)/shard_map/all_gather | solution.py:103
  624.6 11.7 %cholesky.259 = f32[128,128]{1,0:T(8,128)S(1)} custom-call(f32[128,128]{1,0:T(8,128)S(1)} %fusion.52), custom_call_target="Cholesky" | custom-call | tf_op jit(solution)/shard_map/jit(cholesky)/cholesky | solution.py:48
  638.2 9.8 custom-call.37
  648.4 3.6 fusion.108
  657.3 3.8 gather_fusion.11
  667.6 2.9 fusion.115
  671.5 3.1 collective-permute-start.8
  678.6 3.0 collective-permute-done.9
  684.2 3.1 gather_fusion.8
  687.3 3.8 fusion.2
  693.5 3.7 convolution_bitcast_fusion.2
  702.9 124.7 %all-reduce.11.cloned.1.call-done = f32[3,128,128]{2,1,0:T(8,128)} async-done(((f32[3,128,128]{2,1,0:T(8,128)}), f32[3,128,128]{2,1,0:T(8,128)}) %all-reduce.11.cloned.1.call-update) | async-done | bytes 196624 | tf_op jit(solution)/shard_map/psum | solution.py:134
  827.5 3.1 fusion.71
  833.3 3.6 fusion.72
  839.5 3.6 fusion.74
  845.8 4.0 subtract_subtract_fusion
  852.2 4.6 fusion.109
  862.0 3.4 dynamic-slice_select_fusion.1
  865.4 3.7 scatter.36
  872.4 3.4 dynamic-slice_select_fusion
  875.9 3.7 scatter.41
  881.3 33.9 %all-gather.15.cloned.1.call-done = f32[4096,128]{1,0:T(8,128)} async-done(((f32[128,128]{1,0:T(8,128)}), f32[4096,128]{1,0:T(8,128)}) %all-gather.15.cloned.1.call-update) | async-done | bytes 2097168 | tf_op jit(solution)/shard_map/all_gather | solution.py:103
  920.5 13.2 %cholesky.270 = f32[128,128]{1,0:T(8,128)} custom-call(f32[128,128]{1,0:T(8,128)} %fusion.50), custom_call_target="Cholesky" | custom-call | tf_op jit(solution)/shard_map/jit(cholesky)/cholesky | solution.py:48
  947.0 13.2 %cholesky.87 = f32[128,128]{1,0:T(8,128)} custom-call(f32[128,128]{1,0:T(8,128)} %cholesky.279), custom_call_target="Cholesky" | custom-call | tf_op jit(solution)/shard_map/jit(cholesky)/cholesky | solution.py:93
  963.4 11.3 %custom-call.29 = f32[1,128,128]{1,2,0:T(8,128)} custom-call(f32[1,128,128]{2,1,0:T(8,128)} %get-tuple-element.178), custom_call_target="InvertDiagBlocksLowerTriangular" | custom-call | tf_op jit(solution)/shard_map/jit(cholesky)/cholesky | solution.py:93
  979.3 13.2 %cholesky.160 = f32[128,128]{1,0:T(8,128)} custom-call(f32[128,128]{1,0:T(8,128)} %cholesky.283), custom_call_target="Cholesky" | custom-call | tf_op jit(solution)/shard_map/jit(cholesky)/cholesky | solution.py:93
  995.3 11.3 %custom-call.30 = f32[1,128,128]{1,2,0:T(8,128)} custom-call(f32[1,128,128]{2,1,0:T(8,128)} %get-tuple-element.175), custom_call_target="InvertDiagBlocksLowerTriangular" | custom-call | tf_op jit(solution)/shard_map/jit(cholesky)/cholesky | solution.py:93
  1010.2 13.2 %cholesky.179 = f32[128,128]{1,0:T(8,128)} custom-call(f32[128,128]{1,0:T(8,128)} %convolution_subtract_fusion.6), custom_call_target="Cholesky" | custom-call | tf_op jit(solution)/shard_map/jit(cholesky)/cholesky | solution.py:93
  1029.4 10.7 while.11
  1030.0 3.0 bitcast_dynamic-update-slice_fusion.2
  1033.6 3.0 bitcast_dynamic-update-slice_fusion.2
  1037.2 2.9 bitcast_dynamic-update-slice_fusion.2
  1040.1 31.1 %custom-call.31 = f32[3,128,128]{1,2,0:T(8,128)} custom-call(f32[3,128,128]{2,1,0:T(8,128)} %get-tuple-element.132), custom_call_target="InvertDiagBlocksLowerTriangular" | custom-call | tf_op jit(solution)/shard_map/triangular_solve | solution.py:95
  1081.0 10.6 custom-call.38
  (277 shorter events, 198.5 us)
Async XLA Ops:
  7.2 129.7 %copy-start = (bf16[4,320,480]{2,1,0:T(8,128)(2,1)S(1)}, bf16[4,320,480]{2,1,0:T(8,128)(2,1)}, u32[]{:S(2)}) copy-start(bf16[4,320,480]{2,1,0:T(8,128)(2,1)} %param.40) | copy-start | bytes 3686404
  7.2 66.5 %all-gather.9.cloned.1.call-start = ((), (), s32[]{:S(2)}) async-start(), calls=%async_computation.3 | async-start | bytes 2162688 | tf_op jit(solution)/shard_map/all_gather | solution.py:103
  11.9 2.9 copy-start.11
  11.9 3.5 copy-start.34
  11.9 3.6 copy-start.35
  11.9 3.7 copy-start.33
  11.9 4.4 copy-start.32
  14.8 255.1 %all-reduce.7.cloned.1.call-start = ((), (), s32[]{:S(2)}) async-start(), calls=%async_computation | async-start | bytes 131072 | tf_op jit(solution)/shard_map/psum | solution.py:134
  88.5 982.7 %copy-start.27 = (f32[128,128]{0,1:T(8,128)}, f32[128,128]{0,1:T(8,128)S(1)}, u32[]{:S(2)}) copy-start(f32[128,128]{0,1:T(8,128)S(1)} %get-tuple-element.179) | copy-start | bytes 196612
  102.6 1.7 copy-start.9
  117.1 11.6 %collective-permute-start = (bf16[4,80,256]{2,1,0:T(8,128)(2,1)}, bf16[4,80,256]{2,1,0:T(8,128)(2,1)}, u32[]{:S(2)}, u32[]{:S(2)}) collective-permute-start(bf16[4,80,256]{2,1,0:T(8,128)(2,1)} %get-tuple-element.163), channel_id=1, source_target_pairs={{0,4},{4,8},{8,12},{12,16},{16,20},{20,24},{24,28},{1,5},{5,9},{9,... | collective-permute-start | bytes 491528 | tf_op jit(solution)/shard_map/ppermute | solution.py:15
  120.8 9.5 collective-permute-start.1
  123.8 2.9 copy-start.16
  127.8 4.2 collective-permute-start.2
  128.5 4.1 collective-permute-start.3
  130.3 6.6 copy-start.20
  130.3 6.6 copy-start.31
  147.3 194.3 %all-gather.11.cloned.1.call-start = ((), (), s32[]{:S(2)}) async-start(), calls=%async_computation.4 | async-start | bytes 2162688 | tf_op jit(solution)/shard_map/all_gather | solution.py:103
  285.5 258.2 %all-reduce.9.cloned.1.call-start = ((), (), s32[]{:S(2)}) async-start(), calls=%async_computation.1 | async-start | bytes 262144 | tf_op jit(solution)/shard_map/psum | solution.py:134
  386.5 2.9 copy-start.10
  389.4 1.0 copy-start.23
  389.4 5.4 copy-start.15
  390.4 6.6 collective-permute-start.4
  393.4 7.1 collective-permute-start.5
  395.8 5.4 collective-permute-start.6
  396.6 5.3 collective-permute-start.7
  412.3 3.7 copy-start.1
  412.3 3.7 copy-start.13
  418.9 203.8 %all-gather.13.cloned.1.call-start = ((), (), s32[]{:S(2)}) async-start(), calls=%async_computation.5 | async-start | bytes 2162688 | tf_op jit(solution)/shard_map/all_gather | solution.py:103
  546.8 2.7 copy-start.30
  566.2 261.4 %all-reduce.11.cloned.1.call-start = ((), (), s32[]{:S(2)}) async-start(), calls=%async_computation.2 | async-start | bytes 393216 | tf_op jit(solution)/shard_map/psum | solution.py:134
  667.6 2.9 copy-start.8
  670.5 1.0 copy-start.22
  670.5 5.4 copy-start.14
  671.5 6.4 collective-permute-start.8
  674.6 7.1 collective-permute-start.9
  676.9 5.4 collective-permute-start.10
  677.7 5.2 collective-permute-start.11
  693.5 3.7 copy-start.2
  693.5 3.7 copy-start.12
  697.2 2.2 copy-start.5
  702.4 212.7 %all-gather.15.cloned.1.call-start = ((), (), s32[]{:S(2)}) async-start(), calls=%async_computation.6 | async-start | bytes 2162688 | tf_op jit(solution)/shard_map/all_gather | solution.py:103
  830.6 2.7 copy-start.26
  852.2 5.9 copy-start.36
  945.6 0.8 copy-start.21
  978.1 0.7 copy-start.29
  1071.2 3.7 copy-start.25
  1071.2 4.0 copy-start.18
  1072.6 4.4 copy-start.28
  1091.9 2.6 copy-start.24
  1094.5 1.3 copy-start.3
  1095.8 1.3 copy-start.6
  1101.2 2.4 copy-start.4
  1101.2 2.4 copy-start.17
  1103.6 1.3 copy-start.7
  1107.5 1.5 copy-start.19
Sparse Core Ops, SparseCore 0:
  14.9 58.6 all-gather.8
  147.4 122.4 all-reduce.6
  285.6 55.9 all-gather.10
  419.0 124.6 all-reduce.8
  566.3 56.4 all-gather.12
  702.5 124.9 all-reduce.10
  856.9 58.2 all-gather.14
